TPU v7x, 32 devices: a whole 2x2x4 slice. The times are simulated.
32 devices in a mesh: group: 2 (over x), depth: 2 (over core), col: 8 (over z, y).
Axes of the slice: x: 2, y: 2, z: 4, core: 2. Of those that a mesh axis runs over, the one named last changes fastest.
Arguments:
- alignment_activations: bfloat16 [256, 32, 256], P(('group', 'depth'), 'col'), parts along dimension 0, may hold values from -8 to 8
- alignment_mask: int32 [256, 32], P(('group', 'depth'), 'col'), parts along dimension 0, may hold values from 0 to 1, as said below
- pair_activation_input: bfloat16 [64, 32, 128], P(('group', 'col'), 'depth'), parts along dimension 0, may hold values from -6 to 6
- pair_update_mask: int32 [64, 32], P(('group', 'col'), 'depth'), parts along dimension 0, may hold values 0 or 1
- pair_output_gradient: bfloat16 [64, 32, 128], P(('group', 'col'), 'depth'), parts along dimension 0, may hold values from -6 to 6
- layer_scale_factor: float32 [256], replicated, may hold values from 0.25 to 1.75
- first_projector: bfloat16 [256, 32], replicated, may hold values from -0.375 to 0.375
- second_projector: bfloat16 [256, 32], replicated, may hold values from -0.375 to 0.375
- output_weight: bfloat16 [1024, 128], replicated, may hold values from -1.5 to 1.5
- pair_norm_gain: float32 [128], replicated, may hold values from 0.25 to 1.75
- hidden_weight: bfloat16 [128, 512], replicated, may hold values from -0.5 to 0.5
- back_weight: bfloat16 [512, 128], replicated, may hold values from -0.25 to 0.25
Outputs:
- features_derivative: bfloat16 [256, 32, 256], P(('group', 'depth'), 'col'), parts along dimension 0
- couple_features_derivative: bfloat16 [64, 32, 128], P(('group', 'col'), 'depth'), parts along dimension 0
- first_projector_derivative: float32 [512, 32], P('group'), parts along dimension 0
- second_projector_derivative: float32 [512, 32], P('group'), parts along dimension 0
- result_matrix_derivative: float32 [2048, 128], P('group'), parts along dimension 0
- middle_matrix_derivative: float32 [256, 512], P('group'), parts along dimension 0
- final_matrix_derivative: float32 [1024, 128], P('group'), parts along dimension 0
There are 2 independent parts, one for each index of `group`. A program takes and returns all parts, laid end to end along the dimension named above; an argument that names none is the same for every part. Nothing has to cross between parts.
Inputs may be any that keep to these rules, and one draw needn't show every extreme that they name: `alignment_mask`: sequence 0 is present at every residue.
All inputs are finite; a program needn't handle non-finite values. No bound on the sum of `pair_update_mask` on one device may be relied on, other than what follows from the above.
Results may differ from a plain program's by a relative error of at most 0.014.
Values may be sent and summed in bfloat16 or wider, within the bound.
A program may use at most 64 MiB of HBM per device.

v0:
```python
import jax
import jax.numpy as jnp
from jax import lax
from jax.sharding import PartitionSpec as P

epsilon = 1e-05
highest = lax.Precision.HIGHEST


def norm_pieces(entries_drawn):
    center = entries_drawn - jnp.mean(entries_drawn, axis=-1, keepdims=True)
    inv_std = lax.rsqrt(jnp.mean(center * center, axis=-1, keepdims=True) + epsilon)
    return (center * inv_std, inv_std)


def standardize_adjoint(grad_scaled, scaled, inv_std):
    mean_grad = jnp.mean(grad_scaled, axis=-1, keepdims=True)
    mean_cross = jnp.mean(grad_scaled * scaled, axis=-1, keepdims=True)
    return inv_std * (grad_scaled - mean_grad - scaled * mean_cross)


def silu_pieces(pre_act):
    sigma = jax.nn.sigmoid(pre_act)
    return (pre_act * sigma, sigma * (1.0 + pre_act * (1.0 - sigma)))


def on_device(
    alignment_activations,
    alignment_mask,
    pair_activation_input,
    pair_update_mask,
    pair_output_gradient,
    layer_scale_factor,
    first_projector,
    second_projector,
    output_weight,
    pair_norm_gain,
    hidden_weight,
    back_weight,
):
    sequence_row_block, residue_row_block, channel_total = alignment_activations.shape
    proj_width = first_projector.shape[1]
    outer_width = proj_width * proj_width
    depth_count = lax.axis_size("depth")
    residues = residue_row_block * lax.axis_size("col")
    pair_cols = pair_activation_input.shape[1]
    pair_width = pair_activation_input.shape[2]
    col_block = min(64, pair_cols)
    block_count = pair_cols // col_block
    standardized_features, reciprocal_spread = norm_pieces(
        alignment_activations.astype(jnp.float32)
    )
    normalized_rows = (standardized_features * layer_scale_factor).astype(jnp.bfloat16)
    mask_floating = alignment_mask.astype(jnp.float32)
    left_proj = (
        jnp.dot(normalized_rows, first_projector, preferred_element_type=jnp.float32)
        * mask_floating[:, :, None]
    ).astype(jnp.bfloat16)
    right_proj = (
        jnp.dot(normalized_rows, second_projector, preferred_element_type=jnp.float32)
        * mask_floating[:, :, None]
    ).astype(jnp.bfloat16)
    right_flat = right_proj.reshape(sequence_row_block, residue_row_block * proj_width)
    mask_converted = alignment_mask.astype(jnp.bfloat16)
    seq_total = left_proj.shape[0]
    gathered, gathered_mask = (
        lax.all_gather(right_flat, "col", axis=1, tiled=True),
        lax.all_gather(mask_converted, "col", axis=1, tiled=True),
    )
    right_blocks = gathered.reshape(seq_total, depth_count, pair_cols, proj_width)
    mask_blocks = gathered_mask.reshape(seq_total, depth_count, pair_cols)
    block_depth = right_blocks.shape[1]
    out_wide = output_weight.astype(jnp.float32)

    def partial_outer(col_start):
        right_piece = lax.dynamic_slice_in_dim(right_blocks, col_start, col_block, 2)
        outer_part = jnp.einsum(
            "sic,sejd->iejcd", left_proj, right_piece, preferred_element_type=jnp.float32
        )
        return (
            outer_part.reshape(residue_row_block, block_depth, col_block, outer_width),
            right_piece,
        )

    def forward_step(step_index, loop_state):
        projected, pair_count = loop_state
        col_start = step_index * col_block
        outer_part, right_piece = partial_outer(col_start)
        mask_piece = lax.dynamic_slice_in_dim(mask_blocks, col_start, col_block, 2).astype(
            jnp.float32
        )
        count_part = jnp.einsum("si,sej->iej", mask_floating, mask_piece, precision=highest)
        outer_mine, count_mine = (
            lax.psum_scatter(
                outer_part.astype(jnp.bfloat16), "depth", scatter_dimension=1, tiled=True
            ).astype(jnp.float32),
            lax.psum_scatter(
                count_part.astype(jnp.bfloat16), "depth", scatter_dimension=1, tiled=True
            ).astype(jnp.float32),
        )
        proj_mine = jnp.dot(
            outer_mine.reshape(residue_row_block * col_block, outer_width),
            out_wide,
            precision=highest,
        )
        proj_mine = proj_mine.reshape(residue_row_block, col_block, pair_width)
        count_mine = count_mine.reshape(residue_row_block, col_block)
        projected = lax.dynamic_update_slice_in_dim(projected, proj_mine, col_start, 1)
        pair_count = lax.dynamic_update_slice_in_dim(pair_count, count_mine, col_start, 1)
        return (projected, pair_count)

    projected, pair_count = lax.fori_loop(
        0,
        block_count,
        forward_step,
        (
            jnp.zeros((residue_row_block, pair_cols, pair_width), jnp.float32),
            jnp.zeros((residue_row_block, pair_cols), jnp.float32),
        ),
    )
    count_column = pair_count.reshape(residue_row_block * pair_cols, 1)
    mid_act = (
        pair_activation_input.reshape(residue_row_block * pair_cols, pair_width).astype(jnp.float32)
        + projected.reshape(residue_row_block * pair_cols, pair_width) / count_column
    )
    pair_scaled, pair_inv = norm_pieces(mid_act)
    pair_normed = (pair_scaled * pair_norm_gain).astype(jnp.bfloat16)
    pre_act = jnp.dot(pair_normed, hidden_weight, preferred_element_type=jnp.float32)
    act_value, act_slope = silu_pieces(pre_act)
    hidden = act_value.astype(jnp.bfloat16)
    masked_grad = (
        pair_output_gradient * pair_update_mask.astype(jnp.bfloat16)[:, :, None]
    ).reshape(residue_row_block * pair_cols, pair_width)
    final_matrix_derivative = jnp.dot(hidden.T, masked_grad, preferred_element_type=jnp.float32)
    back_prod = jnp.dot(masked_grad, back_weight.T, preferred_element_type=jnp.float32)
    grad_hidden = (back_prod * act_slope).astype(jnp.bfloat16)
    middle_matrix_derivative = jnp.dot(
        pair_normed.T, grad_hidden, preferred_element_type=jnp.float32
    )
    grad_scaled = (
        jnp.dot(grad_hidden, hidden_weight.T, preferred_element_type=jnp.float32) * pair_norm_gain
    )
    grad_mid = pair_output_gradient.reshape(residue_row_block * pair_cols, pair_width).astype(
        jnp.float32
    ) + standardize_adjoint(grad_scaled, pair_scaled, pair_inv)
    couple_features_derivative = grad_mid.astype(jnp.bfloat16).reshape(
        residue_row_block, pair_cols, pair_width
    )
    grad_opm = (
        (grad_mid / count_column)
        .astype(jnp.bfloat16)
        .reshape(residue_row_block, pair_cols, pair_width)
    )
    full_opm = lax.all_gather(grad_opm, "depth", axis=1, tiled=True).reshape(
        residue_row_block, depth_count, pair_cols, pair_width
    )

    def backward_step(step_index, loop_state):
        grad_left_acc, grad_out, right_term = loop_state
        col_start = step_index * col_block
        outer_part, right_piece = partial_outer(col_start)
        opm_piece = lax.dynamic_slice_in_dim(full_opm, col_start, col_block, 2).reshape(
            residue_row_block * block_depth * col_block, pair_width
        )
        grad_out = grad_out + jnp.dot(
            outer_part.reshape(residue_row_block * block_depth * col_block, outer_width).T,
            opm_piece.astype(jnp.float32),
            precision=highest,
        )
        grad_outer = jnp.dot(opm_piece, output_weight.T, preferred_element_type=jnp.float32).astype(
            jnp.bfloat16
        )
        grad_outer = grad_outer.reshape(
            residue_row_block, block_depth, col_block, proj_width, proj_width
        )
        grad_left_acc = grad_left_acc + jnp.einsum(
            "iejcd,sejd->sic", grad_outer, right_piece, preferred_element_type=jnp.float32
        )
        piece_term = jnp.einsum(
            "iejcd,sic->ejsd", grad_outer, left_proj, preferred_element_type=jnp.float32
        )
        piece_term = piece_term.reshape(block_depth, col_block, seq_total * proj_width)
        right_term = lax.dynamic_update_slice_in_dim(right_term, piece_term, col_start, 1)
        return (grad_left_acc, grad_out, right_term)

    grad_left_acc, result_matrix_derivative, right_term = lax.fori_loop(
        0,
        block_count,
        backward_step,
        (
            jnp.zeros((seq_total, residue_row_block, proj_width), jnp.float32),
            jnp.zeros((outer_width, pair_width), jnp.float32),
            jnp.zeros((block_depth, pair_cols, seq_total * proj_width), jnp.float32),
        ),
    )
    grad_right_sum = lax.psum_scatter(
        right_term.reshape(residues, seq_total * proj_width), "col", scatter_dimension=0, tiled=True
    )
    grad_right_acc = jnp.transpose(
        grad_right_sum.reshape(residue_row_block, seq_total, proj_width), (1, 0, 2)
    )
    grad_left = (grad_left_acc * mask_floating[:, :, None]).astype(jnp.bfloat16)
    grad_right = (grad_right_acc * mask_floating[:, :, None]).astype(jnp.bfloat16)
    normed_rows = normalized_rows.reshape(sequence_row_block * residue_row_block, channel_total)
    first_projector_derivative = jnp.dot(
        normed_rows.T,
        grad_left.reshape(sequence_row_block * residue_row_block, proj_width),
        preferred_element_type=jnp.float32,
    )
    second_projector_derivative = jnp.dot(
        normed_rows.T,
        grad_right.reshape(sequence_row_block * residue_row_block, proj_width),
        preferred_element_type=jnp.float32,
    )
    standardized_derivative = jnp.dot(
        grad_left, first_projector.T, preferred_element_type=jnp.float32
    ) + jnp.dot(grad_right, second_projector.T, preferred_element_type=jnp.float32)
    features_derivative = standardize_adjoint(
        standardized_derivative * layer_scale_factor, standardized_features, reciprocal_spread
    ).astype(jnp.bfloat16)
    weight_sums = lax.psum(
        (
            first_projector_derivative,
            second_projector_derivative,
            result_matrix_derivative,
            middle_matrix_derivative,
            final_matrix_derivative,
        ),
        ("depth", "col"),
    )
    return (
        features_derivative,
        couple_features_derivative,
        weight_sums[0],
        weight_sums[1],
        weight_sums[2],
        weight_sums[3],
        weight_sums[4],
    )


def solution(mesh):
    in_specs = (
        P(("group", "depth"), "col", None),
        P(("group", "depth"), "col"),
        P(("group", "col"), "depth", None),
        P(("group", "col"), "depth"),
        P(("group", "col"), "depth", None),
        P(),
        P(),
        P(),
        P(),
        P(),
        P(),
        P(),
    )
    out_specs = (
        P(("group", "depth"), "col", None),
        P(("group", "col"), "depth", None),
        P("group", None),
        P("group", None),
        P("group", None),
        P("group", None),
        P("group", None),
    )
    return jax.shard_map(
        on_device, mesh=mesh, in_specs=in_specs, out_specs=out_specs, check_vma=False
    )
```

profile of v0, /device:TPU:0, one launch (start us, length us, event | category | flops | bytes accessed | tf_op | source)
XLA Modules:
  0.0 362.0 jit_solution(7298277247969911914)
XLA Ops:
  7.2 1.0 convert_reduce_fusion
  8.3 1.1 fusion.16
  9.4 0.8 convert_bitcast_fusion
  10.2 1.2 fusion.4
  11.3 32.6 %all_gather.9 = bf16[64,1024]{0,1:T(8,128)(2,1)S(1)} all-gather(bf16[64,128]{0,1:T(8,128)(2,1)S(1)} %bitcast.138), channel_id=1, replica_groups=mesh['group'=2,'depth'=2,'col'=8] {'col'}, dimensions={1}, use_global_device_ids=true | all-gather | bytes 147456 | tf_op jit(solution)/shard_map/all_gather | solution.py:67
  43.9 1.2 fusion.5
  45.1 1.8 fusion.45
  47.5 1.9 convert_element_type.96
  49.5 20.6 %all-gather = bf16[8,4,64]{2,1,0:T(4,128)(2,1)S(1)} all-gather(bf16[1,4,64]{2,1,0:T(4,128)(2,1)S(1)} %get-tuple-element.95), channel_id=1, replica_groups=mesh['group'=2,'depth'=2,'col'=8] {'col'}, dimensions={0}, use_global_device_ids=true | all-gather | bytes 4608 | tf_op jit(solution)/shard_map/all_gather | solution.py:68
  70.2 2.5 all-reduce.1
  74.6 1.9 copy.35
  76.6 1.0 reshape.170
  78.3 1.6 constant_dynamic-slice_fusion.1
  81.3 0.9 fusion.31
  82.3 0.9 fusion.17
  83.2 0.7 fusion.44
  84.0 1.8 all_gather.11
  86.1 0.8 reshape.166
  88.1 1.2 reshape.167
  89.4 0.9 convolution_bitcast_fusion.4
  90.3 1.4 fusion.47
  91.7 66.1 %all-reduce.12.cloned.1.call-done = f32[32,2048]{1,0:T(8,128)} async-done(((f32[32,2048]{1,0:T(8,128)}), f32[32,2048]{1,0:T(8,128)}) %all-reduce.12.cloned.1.call-update) | async-done | bytes 262160
  157.8 0.8 constant_dynamic-slice_fusion
  158.8 0.9 convolution_bitcast_fusion.3
  160.9 0.8 copy.36
  161.7 85.9 %all-reduce.14.cloned.1.call-done = (f32[256,32]{0,1:T(8,128)}, f32[256,32]{0,1:T(8,128)}) async-done(((f32[256,32]{0,1:T(8,128)}, f32[256,32]{0,1:T(8,128)}), (f32[256,32]{0,1:T(8,128)}, f32[256,32]{0,1:T(8,128)})) %all-reduce.14.cloned.1.call-update) | async-done | bytes 65552 | tf_op jit(solution)/shard_map/psum | solution.py:221
  247.6 99.9 %all-reduce.16.cloned.1.call-done = (f32[1024,128]{1,0:T(8,128)}, f32[128,512]{1,0:T(8,128)}, f32[512,128]{1,0:T(8,128)}) async-done(((f32[1024,128]{1,0:T(8,128)}, f32[128,512]{1,0:T(8,128)}, f32[512,128]{1,0:T(8,128)}), (f32[1024,128]{1,0:T(8,128)}, f32[128,512]{1,0:T(8,128)}, f32[512,128]{1,0:T(8,128)})) %all-reduce.16.cloned.1.call-update) | async-done | bytes 1048592 | tf_op jit(solution)/shard_map/psum | solution.py:221
  347.5 1.4 copy.62
  348.9 1.4 copy.63
  350.3 1.9 copy.64
  352.1 1.7 copy.65
  353.8 1.7 copy.66
  (71 shorter events, 7.2 us)
Async XLA Ops:
  7.2 72.7 %copy-start = (bf16[1024,128]{1,0:T(8,128)(2,1)S(1)}, bf16[1024,128]{1,0:T(8,128)(2,1)}, u32[]{:S(2)}) copy-start(bf16[1024,128]{1,0:T(8,128)(2,1)} %param.20) | copy-start | bytes 786436
  7.2 71.1 %all-reduce.10.cloned.1.call-start = ((), (), s32[]{:S(2)}) async-start(), calls=%async_computation | async-start | bytes 524288
  46.9 23.2 %copy-start.7 = (s32[64,4]{0,1:T(4,128)S(1)}, s32[64,4]{0,1:T(4,128)}, u32[]{:S(2)}) copy-start(s32[64,4]{0,1:T(4,128)} %param.13) | copy-start | bytes 3076
  46.9 25.8 %copy-start.13 = (u32[32]{0:T(128)S(1)}, u32[32]{0:T(128)}, u32[]{:S(2)}) copy-start(u32[32]{0:T(128)} %constant.47) | copy-start | bytes 388
  46.9 27.2 %copy-start.9 = (s32[4,16]{1,0:T(4,128)S(1)}, s32[4,16]{1,0:T(4,128)}, u32[]{:S(2)}) copy-start(s32[4,16]{1,0:T(4,128)} %param.15) | copy-start | bytes 772
  46.9 27.2 %copy-start.12 = (u32[32]{0:T(128)S(1)}, u32[32]{0:T(128)}, u32[]{:S(2)}) copy-start(u32[32]{0:T(128)} %constant.55) | copy-start | bytes 388
  49.4 108.4 %all-reduce.12.cloned.1.call-start = ((), (), s32[]{:S(2)}) async-start(), calls=%async_computation.1 | async-start | bytes 524288
  76.6 1.7 copy-start.4
  76.6 3.5 copy-start.3
  76.6 4.2 %copy-start.2 = (bf16[128,512]{1,0:T(8,128)(2,1)S(1)}, bf16[128,512]{1,0:T(8,128)(2,1)}, u32[]{:S(2)}) copy-start(bf16[128,512]{1,0:T(8,128)(2,1)} %param.22) | copy-start | bytes 393220
  76.6 4.1 %copy-start.8 = (f32[128]{0:T(128)S(1)}, f32[128]{0:T(128)}, u32[]{:S(2)}) copy-start(f32[128]{0:T(128)} %param.21) | copy-start | bytes 1540
  76.6 4.3 %copy-start.11 = (bf16[512,128]{1,0:T(8,128)(2,1)S(1)}, bf16[512,128]{1,0:T(8,128)(2,1)}, u32[]{:S(2)}) copy-start(bf16[512,128]{1,0:T(8,128)(2,1)} %param.23) | copy-start | bytes 393220
  87.3 2.1 copy-start.1
  87.3 2.1 copy-start.10
  88.1 71.7 %copy-start.5 = (bf16[256,32]{0,1:T(8,128)(2,1)S(1)}, bf16[256,32]{0,1:T(8,128)(2,1)}, u32[]{:S(2)}) copy-start(bf16[256,32]{0,1:T(8,128)(2,1)} %param.18) | copy-start | bytes 49156
  89.3 71.0 %copy-start.6 = (bf16[256,32]{0,1:T(8,128)(2,1)S(1)}, bf16[256,32]{0,1:T(8,128)(2,1)}, u32[]{:S(2)}) copy-start(bf16[256,32]{0,1:T(8,128)(2,1)} %param.19) | copy-start | bytes 49156
  89.3 158.3 %all-reduce.14.cloned.1.call-start = ((), (), s32[]{:S(2)}) async-start(), calls=%async_computation.2 | async-start | bytes 131072 | tf_op jit(solution)/shard_map/psum | solution.py:221
  159.7 187.8 %all-reduce.16.cloned.1.call-start = ((), (), s32[]{:S(2)}) async-start(), calls=%async_computation.3 | async-start | bytes 2097152 | tf_op jit(solution)/shard_map/psum | solution.py:221
Sparse Core Ops, SparseCore 0:
  49.5 19.2 all-reduce.9
  89.5 68.2 all-reduce.11
  161.9 85.6 all-reduce.13
  251.8 95.6 all-reduce.15
where the time goes:
time: 363 us; the launch traced here: 362 us
  waiting for transfers between devices  252 us (69%)
  blocking collectives  57.5 us (16%)
  local copies, waits for them, and re-layouts  20.5 us (6%)
  between operations  14.8 us (4%)
  matrix products  11.6 us (3%)
  other arithmetic  5.09 us (1%)
    psum x2, waiting for transfers between devices, on_device(): lax.psum((first_projector_derivative, second_projector_derivative, result...  186 us
    unnamed x6, waiting for transfers between devices  66.5 us
    all_gather x1, blocking collectives, on_device(): lax.all_gather(right_flat, 'col', axis=1, tiled=True)  32.6 us
    all_gather x1, blocking collectives, on_device(): lax.all_gather(mask_converted, 'col', axis=1, tiled=True)  20.6 us
    unnamed x38, local copies, waits for them, and re-layouts  12.4 us
  transfers between devices with their start and end apart: 4, of which 3 were waited for; matrix products, arithmetic and copies ran while one was open for 2% of the time, Pallas kernels for 0%

commit v1 on v0

--- a/solution.py
+++ b/solution.py
@@ -219,14 +219,17 @@
         standardized_derivative * layer_scale_factor, standardized_features, reciprocal_spread
     ).astype(jnp.bfloat16)
     weight_sums = lax.psum(
-        (
-            first_projector_derivative,
-            second_projector_derivative,
-            result_matrix_derivative,
-            middle_matrix_derivative,
-            final_matrix_derivative,
+        lax.psum(
+            (
+                first_projector_derivative,
+                second_projector_derivative,
+                result_matrix_derivative,
+                middle_matrix_derivative,
+                final_matrix_derivative,
+            ),
+            "col",
         ),
-        ("depth", "col"),
+        "depth",
     )
     return (
         features_derivative,

time: 363 us -> 301 us (0.83)
  waiting for transfers between devices: 252 us -> 191 us
    psum x2 -> x1, waiting for transfers between devices: 186 us -> 70.7 us  [on_device(): lax.psum((first_projector_derivative, second_projector_derivative, result...]
    psum x0 -> x2, waiting for transfers between devices: none -> 41 us  [on_device(): lax.psum(lax.psum((first_projector_derivative, second_projector_derivativ...]
    unnamed x6 -> x7, waiting for transfers between devices: 66.5 us -> 79.2 us
  transfers between devices with their start and end apart: 4 -> 5, of which waited for: 3 -> 4; matrix products, arithmetic and copies ran while one was open for 2% -> 3% of each run, Pallas kernels for 0% -> 0%
where the time goes in v1:
time: 301 us; the launch traced here: 300 us
  waiting for transfers between devices  191 us (63%)
  blocking collectives  57.5 us (19%)
  local copies, waits for them, and re-layouts  20.5 us (7%)
  between operations  14.8 us (5%)
  matrix products  11.6 us (4%)
  other arithmetic  5.09 us (2%)
    unnamed x7, waiting for transfers between devices  79.2 us
    psum x1, waiting for transfers between devices, on_device(): lax.psum((first_projector_derivative, second_projector_derivative, result...  70.7 us
    psum x2, waiting for transfers between devices, on_device(): lax.psum(lax.psum((first_projector_derivative, second_projector_derivativ...  41 us
    all_gather x1, blocking collectives, on_device(): lax.all_gather(right_flat, 'col', axis=1, tiled=True)  32.6 us
    all_gather x1, blocking collectives, on_device(): lax.all_gather(mask_converted, 'col', axis=1, tiled=True)  20.6 us
    unnamed x38, local copies, waits for them, and re-layouts  12.4 us
  transfers between devices with their start and end apart: 5, of which 4 were waited for; matrix products, arithmetic and copies ran while one was open for 3% of the time, Pallas kernels for 0%

profile of v1, /device:TPU:0, one launch (start us, length us, event | category | flops | bytes accessed | tf_op | source)
XLA Modules:
  0.0 300.5 jit_solution(3781440945031168000)
XLA Ops:
  7.2 1.0 convert_reduce_fusion
  8.3 1.1 fusion.16
  9.4 0.8 convert_bitcast_fusion
  10.2 1.2 fusion.4
  11.3 32.6 %all_gather.9 = bf16[64,1024]{0,1:T(8,128)(2,1)S(1)} all-gather(bf16[64,128]{0,1:T(8,128)(2,1)S(1)} %bitcast.138), channel_id=1, replica_groups=mesh['group'=2,'depth'=2,'col'=8] {'col'}, dimensions={1}, use_global_device_ids=true | all-gather | bytes 147456 | tf_op jit(solution)/shard_map/all_gather | solution.py:67
  43.9 1.2 fusion.5
  45.1 1.8 fusion.45
  47.5 1.8 convert_element_type.96
  49.4 20.6 %all-gather = bf16[8,4,64]{2,1,0:T(4,128)(2,1)S(1)} all-gather(bf16[1,4,64]{2,1,0:T(4,128)(2,1)S(1)} %get-tuple-element.101), channel_id=1, replica_groups=mesh['group'=2,'depth'=2,'col'=8] {'col'}, dimensions={0}, use_global_device_ids=true | all-gather | bytes 4608 | tf_op jit(solution)/shard_map/all_gather | solution.py:68
  70.1 2.5 all-reduce.1
  73.9 1.9 copy.35
  75.9 1.0 reshape.170
  77.0 1.6 constant_dynamic-slice_fusion.1
  80.0 0.9 fusion.31
  80.9 0.9 fusion.17
  82.7 1.8 all_gather.11
  84.7 1.4 fusion.47
  86.1 0.8 reshape.166
  87.7 1.2 reshape.167
  90.7 0.9 convolution_bitcast_fusion.4
  91.6 78.6 %all-reduce.17.cloned.1.call-done = (f32[32,2048]{1,0:T(8,128)}, f32[1024,128]{1,0:T(8,128)}, f32[128,512]{1,0:T(8,128)}, f32[512,128]{1,0:T(8,128)}) async-done(((f32[32,2048]{1,0:T(8,128)}, f32[1024,128]{1,0:T(8,128)}, f32[128,512]{1,0:T(8,128)}, f32[512,128]{1,0:T(8,128)}), (f32[32,2048]{1,0:T(8,128)}, f32[1024,128]{1,0:T(8,128)}, f32[128,512]{1,0:T(8,128)}, ...) | async-done | bytes 1310736
  170.2 0.8 constant_dynamic-slice_fusion
  171.2 0.9 convolution_bitcast_fusion.3
  172.2 70.7 %all-reduce.15.cloned.1.call-done = (f32[256,32]{0,1:T(8,128)}, f32[256,32]{0,1:T(8,128)}) async-done(((f32[256,32]{0,1:T(8,128)}, f32[256,32]{0,1:T(8,128)}), (f32[256,32]{0,1:T(8,128)}, f32[256,32]{0,1:T(8,128)})) %all-reduce.15.cloned.1.call-update) | async-done | bytes 65552 | tf_op jit(solution)/shard_map/psum | solution.py:222
  244.2 0.8 copy.36
  245.0 17.8 %all-reduce.19.cloned.1.call-done = (f32[256,32]{0,1:T(8,128)}, f32[256,32]{0,1:T(8,128)}) async-done(((f32[256,32]{0,1:T(8,128)}, f32[256,32]{0,1:T(8,128)}), (f32[256,32]{0,1:T(8,128)}, f32[256,32]{0,1:T(8,128)})) %all-reduce.19.cloned.1.call-update) | async-done | bytes 65552 | tf_op jit(solution)/shard_map/psum | solution.py:221
  262.8 23.2 %all-reduce.21.cloned.1.call-done = (f32[1024,128]{1,0:T(8,128)}, f32[128,512]{1,0:T(8,128)}, f32[512,128]{1,0:T(8,128)}) async-done(((f32[1024,128]{1,0:T(8,128)}, f32[128,512]{1,0:T(8,128)}, f32[512,128]{1,0:T(8,128)}), (f32[1024,128]{1,0:T(8,128)}, f32[128,512]{1,0:T(8,128)}, f32[512,128]{1,0:T(8,128)})) %all-reduce.21.cloned.1.call-update) | async-done | bytes 1048592 | tf_op jit(solution)/shard_map/psum | solution.py:221
  286.0 1.4 copy.67
  287.4 1.4 copy.68
  288.8 1.9 copy.69
  290.6 1.7 copy.70
  292.3 1.7 copy.71
  (74 shorter events, 8.2 us)
Async XLA Ops:
  7.2 71.4 %copy-start = (bf16[1024,128]{1,0:T(8,128)(2,1)S(1)}, bf16[1024,128]{1,0:T(8,128)(2,1)}, u32[]{:S(2)}) copy-start(bf16[1024,128]{1,0:T(8,128)(2,1)} %param.20) | copy-start | bytes 786436
  7.2 69.8 %all-reduce.13.cloned.1.call-start = ((), (), s32[]{:S(2)}) async-start(), calls=%async_computation | async-start | bytes 524288
  46.8 23.1 %copy-start.7 = (s32[64,4]{0,1:T(4,128)S(1)}, s32[64,4]{0,1:T(4,128)}, u32[]{:S(2)}) copy-start(s32[64,4]{0,1:T(4,128)} %param.13) | copy-start | bytes 3076
  46.8 25.8 %copy-start.13 = (u32[32]{0:T(128)S(1)}, u32[32]{0:T(128)}, u32[]{:S(2)}) copy-start(u32[32]{0:T(128)} %constant.47) | copy-start | bytes 388
  46.8 27.1 %copy-start.9 = (s32[4,16]{1,0:T(4,128)S(1)}, s32[4,16]{1,0:T(4,128)}, u32[]{:S(2)}) copy-start(s32[4,16]{1,0:T(4,128)} %param.15) | copy-start | bytes 772
  49.3 120.9 %all-reduce.17.cloned.1.call-start = ((), (), s32[]{:S(2)}) async-start(), calls=%async_computation.2 | async-start | bytes 2621440
  75.9 1.0 copy-start.4
  75.9 2.9 copy-start.3
  75.9 3.5 %copy-start.2 = (bf16[128,512]{1,0:T(8,128)(2,1)S(1)}, bf16[128,512]{1,0:T(8,128)(2,1)}, u32[]{:S(2)}) copy-start(bf16[128,512]{1,0:T(8,128)(2,1)} %param.22) | copy-start | bytes 393220
  75.9 3.5 %copy-start.8 = (f32[128]{0:T(128)S(1)}, f32[128]{0:T(128)}, u32[]{:S(2)}) copy-start(f32[128]{0:T(128)} %param.21) | copy-start | bytes 1540
  75.9 3.6 %copy-start.11 = (bf16[512,128]{1,0:T(8,128)(2,1)S(1)}, bf16[512,128]{1,0:T(8,128)(2,1)}, u32[]{:S(2)}) copy-start(bf16[512,128]{1,0:T(8,128)(2,1)} %param.23) | copy-start | bytes 393220
  87.3 1.7 copy-start.12
  87.7 3.0 copy-start.1
  87.7 3.0 copy-start.10
  89.0 154.5 %copy-start.5 = (bf16[256,32]{0,1:T(8,128)(2,1)S(1)}, bf16[256,32]{0,1:T(8,128)(2,1)}, u32[]{:S(2)}) copy-start(bf16[256,32]{0,1:T(8,128)(2,1)} %param.18) | copy-start | bytes 49156
  89.0 153.8 %all-reduce.15.cloned.1.call-start = ((), (), s32[]{:S(2)}) async-start(), calls=%async_computation.1 | async-start | bytes 131072 | tf_op jit(solution)/shard_map/psum | solution.py:222
  90.3 153.4 %copy-start.6 = (bf16[256,32]{0,1:T(8,128)(2,1)S(1)}, bf16[256,32]{0,1:T(8,128)(2,1)}, u32[]{:S(2)}) copy-start(bf16[256,32]{0,1:T(8,128)(2,1)} %param.19) | copy-start | bytes 49156
  172.1 90.7 %all-reduce.19.cloned.1.call-start = ((), (), s32[]{:S(2)}) async-start(), calls=%async_computation.3 | async-start | bytes 131072 | tf_op jit(solution)/shard_map/psum | solution.py:221
  242.8 43.2 %all-reduce.21.cloned.1.call-start = ((), (), s32[]{:S(2)}) async-start(), calls=%async_computation.4 | async-start | bytes 2097152 | tf_op jit(solution)/shard_map/psum | solution.py:221
Sparse Core Ops, SparseCore 0:
  49.4 19.2 all-reduce.12
  89.1 81.0 all-reduce.16
  174.3 68.5 all-reduce.14
  245.0 17.7 all-reduce.18
  265.1 20.8 all-reduce.20
